TPU v7x, 32 devices: a whole 2x2x4 slice. The times are simulated.
32 devices in a mesh: pix: 4 (over y, core), chan: 8 (over z, x).
Axes of the slice: x: 2, y: 2, z: 4, core: 2. Of those that a mesh axis runs over, the one named last changes fastest.
Arguments:
- images: bfloat16 [2048, 32, 128], P('pix', 'chan'), may hold values from -6 to 6
- conv_weight: float32 [2048, 49], P('pix'), may hold values from -6 to 6
- conv_bias: float32 [2048], P('pix'), may hold values from -4 to 4
- norm_gain: float32 [2048], replicated, may hold values from 0.25 to 1.75
- norm_shift: float32 [2048], replicated, may hold values from -3 to 3
- up_weight: bfloat16 [2048, 8192], P(None, 'pix'), may hold values from -0.125 to 0.125
- up_bias: float32 [8192], P('pix'), may hold values from -3 to 3
- down_weight: bfloat16 [2048, 8192], P(None, 'pix'), may hold values from -0.09375 to 0.09375
- down_bias: float32 [2048], P('pix'), may hold values from -3 to 3
- layer_scale: float32 [2048], P('pix'), may hold values from 0.5 to 2
Outputs:
- block_out: bfloat16 [2048, 32, 128], P('pix', 'chan')
All inputs are finite; a program needn't handle non-finite values.
Results may differ from a plain program's by a relative error of at most 0.006.
Values may be sent and summed in bfloat16 or wider, within the bound.
A program may use at most 64 MiB of HBM per device.

v0:
```python
import jax
import jax.numpy as jnp
from jax import lax
from jax.sharding import PartitionSpec as P

C = 2048


def with_halo(block, sides, width):
    for axis, dim in sides:
        count = lax.axis_size(axis)
        forward = [(i, i + 1) for i in range(count - 1)]
        backward = [(target, source) for source, target in forward]
        low = lax.ppermute(
            lax.slice_in_dim(block, block.shape[dim] - width, None, axis=dim), axis, forward
        )
        high = lax.ppermute(lax.slice_in_dim(block, 0, width, axis=dim), axis, backward)
        block = jnp.concatenate([low, block, high], axis=dim)
    return block


def on_device(
    images,
    conv_weight,
    conv_bias,
    norm_gain,
    norm_shift,
    up_weight,
    up_bias,
    down_weight,
    down_bias,
    layer_scale,
):
    chans, rows, width = images.shape
    pixels = rows * width
    padded = with_halo(images, (("chan", 1),), 3)
    wide = jnp.pad(padded.astype(jnp.float32), ((0, 0), (0, 0), (3, 3)))
    total = jnp.zeros((chans, rows, width), jnp.float32)
    for first in range(7):
        for second in range(7):
            total = (
                total
                + conv_weight[:, first * 7 + second][:, None, None]
                * wide[:, first : first + rows, second : second + width]
            )
    filtered = (total + conv_bias[:, None, None]).astype(jnp.bfloat16).reshape(chans, pixels)
    values = filtered.astype(jnp.float32)
    sum_first, sum_second = lax.psum(
        (jnp.sum(values, axis=0), jnp.sum(values * values, axis=0)), "pix"
    )
    mean = sum_first / C
    var = sum_second / C - mean * mean
    offset = lax.axis_index("pix") * chans
    gain_local = lax.dynamic_slice_in_dim(norm_gain, offset, chans, 0)
    shift_local = lax.dynamic_slice_in_dim(norm_shift, offset, chans, 0)
    normed_local = (
        (values - mean) * lax.rsqrt(var + 1e-06) * gain_local[:, None] + shift_local[:, None]
    ).astype(jnp.bfloat16)
    gathered = lax.all_gather(normed_local, "pix", axis=0, tiled=True)
    contract = (((0,), (0,)), ((), ()))
    pre = lax.dot_general(up_weight, gathered, contract, preferred_element_type=jnp.float32)
    hidden = jax.nn.gelu(pre + up_bias[:, None], approximate=True).astype(jnp.bfloat16)
    terms = jnp.dot(down_weight, hidden, preferred_element_type=jnp.float32)
    mixed = lax.psum_scatter(terms, "pix", scatter_dimension=0, tiled=True)
    result = images.astype(jnp.float32).reshape(chans, pixels) + layer_scale[:, None] * (
        mixed + down_bias[:, None]
    )
    return result.astype(jnp.bfloat16).reshape(chans, rows, width)


def solution(mesh):
    placed = (
        P("pix", "chan", None),
        P("pix", None),
        P("pix"),
        P(),
        P(),
        P(None, "pix"),
        P("pix"),
        P(None, "pix"),
        P("pix"),
        P("pix"),
    )
    return jax.shard_map(
        on_device, mesh=mesh, in_specs=placed, out_specs=P("pix", "chan", None), check_vma=False
    )
```

profile of v0, /device:TPU:3, one launch (start us, length us, event | category | flops | bytes accessed | tf_op | source)
XLA Modules:
  0.0 192.9 jit_solution(2396810698593595446)
XLA Ops:
  6.5 0.0 copy-start.3
  6.5 0.0 all-gather.2.cloned.1.call-start
  6.5 1.7 fusion.103
  8.2 3.2 %collective-permute-start = (bf16[512,3,128]{2,1,0:T(4,128)(2,1)S(1)}, bf16[512,3,128]{2,1,0:T(4,128)(2,1)S(1)}, u32[]{:S(2)}, u32[]{:S(2)}) collective-permute-start(bf16[512,3,128]{2,1,0:T(4,128)(2,1)S(1)} %get-tuple-element.10), channel_id=1, source_target_pairs={{0,1},{1,2},{2,3},{3,4},{4,5},{5,6},{6,7},{8,9},{9,10},{10,11},{11... | collective-permute-start | bytes 1179656 | tf_op jit(solution)/shard_map/ppermute | solution.py:14
  11.4 2.1 %collective-permute-start.1 = (bf16[512,3,128]{2,1,0:T(4,128)(2,1)S(1)}, bf16[512,3,128]{2,1,0:T(4,128)(2,1)S(1)}, u32[]{:S(2)}, u32[]{:S(2)}) collective-permute-start(bf16[512,3,128]{2,1,0:T(4,128)(2,1)S(1)} %get-tuple-element.11), channel_id=1, source_target_pairs={{1,0},{2,1},{3,2},{4,3},{5,4},{6,5},{7,6},{9,8},{10,9},{11,10},{12... | collective-permute-start | bytes 1179656 | tf_op jit(solution)/shard_map/ppermute | solution.py:17
  13.6 1.1 fusion.104
  14.7 0.8 dynamic_slice.6
  15.5 0.8 dynamic_slice.7
  16.2 1.0 fusion.106
  17.2 1.2 fusion.105
  18.4 15.8 %collective-permute-done = bf16[512,3,128]{2,1,0:T(4,128)(2,1)S(1)} collective-permute-done((bf16[512,3,128]{2,1,0:T(4,128)(2,1)S(1)}, bf16[512,3,128]{2,1,0:T(4,128)(2,1)S(1)}, u32[]{:S(2)}, u32[]{:S(2)}) %collective-permute-start) | collective-permute-done | bytes 393248 | tf_op jit(solution)/shard_map/ppermute | solution.py:14
  34.2 0.0 collective-permute-done.1
  34.2 2.2 %maximum_convert_fusion = f32[512,10,128]{2,1,0:T(8,128)S(1)} fusion(bf16[512,3,128]{2,1,0:T(4,128)(2,1)S(1)} %collective-permute-done.1, bf16[512,4,128]{2,1,0:T(4,128)(2,1)} %param.10, bf16[512,3,128]{2,1,0:T(4,128)(2,1)S(1)} %collective-permute-done), kind=kLoop, calls=%fused_computation.52 | loop fusion | flops 3932160 | bytes 3932160 | tf_op jit(solution)/shard_map/convert_element_type | solution.py:37
  36.4 0.0 copy-done.3
  36.4 0.0 copy-start.4
  36.4 52.7 %convert_reduce_fusion = (f32[4,128]{1,0:T(4,128)S(1)}, f32[4,128]{1,0:T(4,128)S(1)}, bf16[512,4,128]{2,1,0:T(4,128)(2,1)S(1)}) fusion(f32[512]{0:T(512)S(1)} %copy-done.3, f32[512]{0:T(512)S(1)} %bitcast.118, f32[512]{0:T(512)S(1)} %bitcast.119, f32[512]{0:T(512)S(1)} %bitcast.91, f32[512,10,128]{2,1,0:T(8,128)S(1)} %maximum_convert_fusion, ...), kind=kLoop, calls=%fused_computation.159 | loop fusion | flops 26999808 | bytes 12165120 | tf_op jit(solution)/shard_map/reduce_sum | solution.py:49
  89.1 0.1 convert.2
  89.2 6.5 %all-reduce.1 = (f32[512]{0:T(512)S(1)}, f32[512]{0:T(512)S(1)}) all-reduce(f32[512]{0:T(512)S(1)} %bitcast.140, f32[512]{0:T(512)S(1)} %bitcast.139), channel_id=1, replica_groups=mesh['pix'=4,'chan'=8] {'pix'}, use_global_device_ids=true, to_apply=%region_3.4 | all-reduce | flops 1024 | bytes 8192 | tf_op jit(solution)/shard_map/psum | solution.py:48
  95.8 1.0 fusion.101
  96.8 0.0 all-gather.2.cloned.1.call-update
  96.8 0.2 reduce-scatter.2.cloned.1.call-start
  97.1 24.3 %all-gather.2.cloned.1.call-done = bf16[2048,512]{1,0:T(8,128)(2,1)} async-done(((bf16[512,512]{1,0:T(8,128)(2,1)}), bf16[2048,512]{1,0:T(8,128)(2,1)}) %all-gather.2.cloned.1.call-update) | async-done | bytes 2097168 | tf_op jit(solution)/shard_map/all_gather | solution.py:59
  121.4 0.0 copy-done.4
  121.4 18.1 %convolution_bitcast_fusion = f32[2048,512]{0,1:T(8,128)} fusion(bf16[2048,2048]{1,0:T(8,128)(2,1)} %param.17, bf16[2048,512]{1,0:T(8,128)(2,1)} %all-gather.2.cloned.1.call-done, bf16[2048,2048]{1,0:T(8,128)(2,1)} %param.15, f32[2048]{0:T(1024)S(1)} %copy-done.4), kind=kOutput, calls=%fused_computation.51 | convolution fusion | flops 8600420352 | bytes 23076864 | tf_op jit(solution)/shard_map/dot_general | solution.py:63
  139.5 0.0 copy-start
  139.5 0.0 copy-start.1
  139.5 0.0 copy-start.2
  139.5 0.0 reduce-scatter.2.cloned.1.call-update
  139.5 1.0 copy-done
  140.5 0.3 copy.11
  140.8 42.7 %reduce-scatter.2.cloned.1.call-done = f32[512,512]{0,1:T(8,128)} async-done(((f32[2048,512]{0,1:T(8,128)}), f32[512,512]{0,1:T(8,128)}) %reduce-scatter.2.cloned.1.call-update) | async-done | bytes 1048592 | tf_op jit(solution)/shard_map/reduce_scatter | solution.py:64
  183.5 0.0 copy-done.1
  183.5 0.0 copy-done.2
  183.5 1.5 fusion.102
  185.0 1.1 copy.12
  (1 shorter events, 0.0 us)
Async XLA Ops:
  6.5 29.8 %copy-start.3 = (f32[512]{0:T(512)S(1)}, f32[512]{0:T(512)}, u32[]{:S(2)}) copy-start(f32[512]{0:T(512)} %param.12) | copy-start | bytes 6148
  6.5 114.8 %all-gather.2.cloned.1.call-start = ((), (), s32[]{:S(2)}) async-start(), calls=%async_computation.1 | async-start | bytes 2621440 | tf_op jit(solution)/shard_map/all_gather | solution.py:59
  8.2 25.9 %collective-permute-start = (bf16[512,3,128]{2,1,0:T(4,128)(2,1)S(1)}, bf16[512,3,128]{2,1,0:T(4,128)(2,1)S(1)}, u32[]{:S(2)}, u32[]{:S(2)}) collective-permute-start(bf16[512,3,128]{2,1,0:T(4,128)(2,1)S(1)} %get-tuple-element.10), channel_id=1, source_target_pairs={{0,1},{1,2},{2,3},{3,4},{4,5},{5,6},{6,7},{8,9},{9,10},{10,11},{11... | collective-permute-start | bytes 1179656 | tf_op jit(solution)/shard_map/ppermute | solution.py:14
  11.4 22.8 %collective-permute-start.1 = (bf16[512,3,128]{2,1,0:T(4,128)(2,1)S(1)}, bf16[512,3,128]{2,1,0:T(4,128)(2,1)S(1)}, u32[]{:S(2)}, u32[]{:S(2)}) collective-permute-start(bf16[512,3,128]{2,1,0:T(4,128)(2,1)S(1)} %get-tuple-element.11), channel_id=1, source_target_pairs={{1,0},{2,1},{3,2},{4,3},{5,4},{6,5},{7,6},{9,8},{10,9},{11,10},{12... | collective-permute-start | bytes 1179656 | tf_op jit(solution)/shard_map/ppermute | solution.py:17
  36.4 85.0 %copy-start.4 = (f32[2048]{0:T(1024)S(1)}, f32[2048]{0:T(1024)}, u32[]{:S(2)}) copy-start(f32[2048]{0:T(1024)} %param.16) | copy-start | bytes 24580
  96.8 86.7 %reduce-scatter.2.cloned.1.call-start = ((), (), s32[]{:S(2)}) async-start(), calls=%async_computation.2 | async-start | bytes 5242880 | tf_op jit(solution)/shard_map/reduce_scatter | solution.py:64
  139.5 1.0 copy-start
  139.5 44.1 %copy-start.1 = (f32[512]{0:T(512)S(1)}, f32[512]{0:T(512)}, u32[]{:S(2)}) copy-start(f32[512]{0:T(512)} %param.18) | copy-start | bytes 6148
  139.5 44.1 %copy-start.2 = (f32[512]{0:T(512)S(1)}, f32[512]{0:T(512)}, u32[]{:S(2)}) copy-start(f32[512]{0:T(512)} %param.19) | copy-start | bytes 6148
Sparse Core Ops, SparseCore 0:
  97.0 24.3 all-gather.1
  139.6 43.8 reduce-scatter.1
where the time goes:
time: 195 us; the launch traced here: 193 us
  waiting for transfers between devices  82.9 us (43%)
  other arithmetic  57.5 us (29%)
  matrix products  18.1 us (9%)
  between operations  13.5 us (7%)
  local copies, waits for them, and re-layouts  8.88 us (5%)
  blocking collectives  6.55 us (3%)
  starting transfers between devices  5.54 us (3%)
    reduce_sum x1, other arithmetic, on_device(): jnp.sum(values, axis=0)  52.7 us
    reduce_scatter x1, waiting for transfers between devices, on_device(): mixed = lax.psum_scatter(terms, 'pix', scatter_dimension=0, tiled=True)  42.7 us
    all_gather x1, waiting for transfers between devices, on_device(): gathered = lax.all_gather(normed_local, 'pix', axis=0, tiled=True)  24.3 us
    dot_general x1, matrix products, on_device(): terms = jnp.dot(down_weight, hidden, preferred_element_type=jnp.float32)  18.1 us
    ppermute x1, waiting for transfers between devices, with_halo(): lax.ppermute(lax.slice_in_dim(block, block.shape[dim] - width, None, axis...  15.8 us
    psum x1, blocking collectives, on_device(): lax.psum((jnp.sum(values, axis=0), jnp.sum(values * values, axis=0)), 'pix')  6.55 us
  transfers between devices with their start and end apart: 4, of which 3 were waited for; matrix products, arithmetic and copies ran while one was open for 3% of the time, Pallas kernels for 0%

commit v1 on v0

v1 whole, which is shorter than its diff:
```python
import functools

import jax
import jax.numpy as jnp
from jax import lax
from jax.experimental import pallas as pl
from jax.experimental.pallas import tpu as pltpu
from jax.sharding import PartitionSpec as P

MESH = pl.DeviceIdType.MESH
LANES = 128
TAPS = 7
HALO = 3
EDGE = 8
STRIP = 16


def kernel(
    n, m, x_ref, taps_ref, cbias_ref, gain_ref, shift_ref, ubias_ref, up_hbm, down_hbm, out_ref,
    up, down, near, far, wide, gath, normed, hidden, half_out, half_in, kept, cross_out, cross_in,
    up_sem, down_sem, near_send, near_recv, far_send, far_recv,
    gath_send, fwd_send, gath_recv, half_send, half_recv, cross_send, cross_recv,
):
    chunks, rows, width, _ = x_ref.shape
    pixels = rows * width
    chips = n // 2
    channels = n * chunks * LANES
    block = channels // n
    steps, sub = half_out.shape[0], half_out.shape[1]
    per_chip = steps // chips
    far_steps = steps - per_chip
    pix = lax.axis_index("pix")
    chan = lax.axis_index("chan")
    chip, core = pix // 2, pix % 2
    odd = chan % 2
    beside = chan + 1 - 2 * odd
    onward = chan + 2 - 4 * odd
    behind = chan - 2 + 4 * odd
    has_onward = (onward >= 0) & (onward < m)
    has_behind = (behind >= 0) & (behind < m)
    partner = pix + 1 - 2 * core

    def other(step):
        return ((chip + 1 + step) % chips) * 2 + core

    barrier = pltpu.get_barrier_semaphore()

    def greet(to_pix, to_chan):
        pl.semaphore_signal(
            barrier, inc=1, device_id={"pix": to_pix, "chan": to_chan}, device_id_type=MESH
        )

    greet(pix, beside)
    greet(partner, chan)
    for step in range(chips - 1):
        greet(other(step), chan)

    @pl.when(has_onward)
    def _():
        greet(pix, onward)

    @pl.when(has_behind)
    def _():
        greet(pix, behind)

    up_copy = pltpu.make_async_copy(up_hbm, up, up_sem)
    down_copy = pltpu.make_async_copy(down_hbm, down, down_sem)
    wide[...] = jnp.zeros_like(wide)

    @pl.when(jnp.logical_not(has_behind))
    def _():
        far[...] = jnp.zeros_like(far)

    pl.semaphore_wait(
        barrier, 1 + chips + has_onward.astype(jnp.int32) + has_behind.astype(jnp.int32)
    )

    def remote(src, dst, send, recv, to_pix, to_chan):
        return pltpu.make_async_remote_copy(
            src_ref=src, dst_ref=dst, send_sem=send, recv_sem=recv,
            device_id={"pix": to_pix, "chan": to_chan}, device_id_type=MESH,
        )

    def near_copy(k):
        return remote(x_ref.at[k], near.at[k], near_send.at[k], near_recv.at[k], pix, beside)

    def far_copy(k):
        return remote(
            near.at[k, pl.ds(1 - odd, HALO)], far.at[k], far_send.at[k], far_recv.at[k], pix, onward
        )

    def own_copy(k, step):
        slot = gath.at[pix * chunks + k]
        to = partner if step == chips - 1 else other(step)
        return remote(
            slot, slot, gath_send.at[step * chunks + k], gath_recv.at[pix * chunks + k], to, chan
        )

    def arrival(slot):
        return remote(gath.at[slot], gath.at[slot], up_sem, gath_recv.at[slot], partner, chan)

    def forward_copy(k, step):
        index = other(step) * chunks + k
        slot = gath.at[index]
        return remote(slot, slot, fwd_send.at[step * chunks + k], gath_recv.at[index], partner, chan)

    for k in range(chunks):
        near_copy(k).start()
    up_copy.start()
    down_copy.start()

    def pass_on(k):
        near_copy(k).wait_recv()

        @pl.when(has_onward)
        def _():
            far_copy(k).start()

    def filter_chunk(k):
        @pl.when(has_behind)
        def _():
            far_copy(k).wait_recv()

        inner = pl.ds(EDGE, width)
        wide[HALO : HALO + rows, inner, :] = x_ref[k].astype(jnp.float32)
        wide[pl.ds((HALO + rows) * (1 - odd), HALO), inner, :] = near[k, pl.ds(odd * (rows - HALO), HALO)].astype(
            jnp.float32
        )
        wide[pl.ds((HALO + rows) * odd, HALO), inner, :] = far[k].astype(jnp.float32)
        bias = cbias_ref[k]
        own = pix * chunks + k

        def strip(s, carry):
            first = pl.multiple_of(s * STRIP, STRIP)
            sums = [jnp.zeros((STRIP, LANES), jnp.float32) for _ in range(rows)]
            for b in range(TAPS):
                for i in range(rows + TAPS - 1):
                    piece = wide[i, pl.ds(first + (EDGE - HALO + b), STRIP), :]
                    for o in range(rows):
                        a = i - o
                        if 0 <= a < TAPS:
                            tap = a * TAPS + b
                            sums[o] = sums[o] + taps_ref[k, tap : tap + 1, :] * piece
            for o in range(rows):
                gath[own, pl.ds(pl.multiple_of(o * width + first, STRIP), STRIP), :] = (
                    sums[o] + bias
                ).astype(jnp.bfloat16)
            return carry

        lax.fori_loop(0, width // STRIP, strip, 0)
        for step in range(chips):
            own_copy(k, step).start()

    def relay(k):
        for step in range(chips - 1):
            arrival(other(step) * chunks + k).wait_recv()
            forward_copy(k, step).start()

    def front(k, carry):
        @pl.when(k < chunks)
        def _():
            pass_on(k)

        @pl.when((k >= 1) & (k < chunks + 1))
        def _():
            filter_chunk(k - 1)

        @pl.when(k >= 2)
        def _():
            relay(k - 2)

        return carry

    lax.fori_loop(0, chunks + 2, front, 0)

    def settle(k, carry):
        arrival(partner * chunks + k).wait_recv()
        for step in range(chips - 1):
            mate = other(step) + 1 - 2 * core
            arrival(mate * chunks + k).wait_recv()
        return carry

    lax.fori_loop(0, chunks, settle, 0)

    band = 64
    slots = n * chunks

    def normalise(s, carry):
        here = pl.ds(pl.multiple_of(s * band, band), band)
        first = jnp.zeros((band, LANES), jnp.float32)
        second = jnp.zeros((band, LANES), jnp.float32)
        for q in range(slots):
            v = gath[q, here, :].astype(jnp.float32)
            first = first + v
            second = second + v * v
        mean = jnp.sum(first, axis=1, keepdims=True) / channels
        var = jnp.sum(second, axis=1, keepdims=True) / channels - mean * mean
        scale = lax.rsqrt(var + 1e-06)
        for q in range(slots):
            lanes = slice(q * LANES, (q + 1) * LANES)
            v = gath[q, here, :].astype(jnp.float32)
            normed[here, lanes] = (
                (v - mean) * scale * gain_ref[:, lanes] + shift_ref[:, lanes]
            ).astype(jnp.bfloat16)
        return carry

    lax.fori_loop(0, pixels // band, normalise, 0)

    up_copy.wait()
    units = up.shape[1]
    tile = 256

    def expand(s, carry):
        cols = pl.ds(pl.multiple_of(s * tile, tile), tile)
        v = jnp.dot(normed[...], up[:, cols], preferred_element_type=jnp.float32) + ubias_ref[:, cols]
        hidden[:, cols] = (
            0.5 * v * (1.0 + jnp.tanh(0.7978845608 * (v + 0.044715 * (v * v * v))))
        ).astype(jnp.bfloat16)
        return carry

    lax.fori_loop(0, units // tile, expand, 0)

    down_copy.wait()

    def half_copy(t):
        return remote(half_out.at[t], half_in.at[t], half_send.at[t], half_recv.at[t], partner, chan)

    def cross_copy(t):
        return remote(
            cross_out.at[t], cross_in.at[t], cross_send.at[t], cross_recv.at[t],
            other(t // per_chip), chan,
        )

    def contract(start):
        part = down[pl.ds(pl.multiple_of(start, sub), sub), :]
        return lax.dot_general(
            part, hidden[...], (((1,), (1,)), ((), ())), preferred_element_type=jnp.float32
        )

    def combine(t):
        half_copy(t).wait_recv()

        @pl.when(t < far_steps)
        def _():
            cross_out[t] = (kept[t] + half_in[t].astype(jnp.float32)).astype(jnp.bfloat16)
            cross_copy(t).start()

        @pl.when(t >= far_steps)
        def _():
            kept[t] = kept[t] + half_in[t].astype(jnp.float32)

    def reduce(t, carry):
        @pl.when(t < steps)
        def _():
            owner = other(t // per_chip)
            away = owner + 1 - 2 * core
            row = (t % per_chip) * sub
            half_out[t] = contract(away * block + row).astype(jnp.bfloat16)
            half_copy(t).start()
            kept[t] = contract(owner * block + row)

        @pl.when(t >= 1)
        def _():
            combine(t - 1)

        return carry

    lax.fori_loop(0, steps + 1, reduce, 0)

    def finish(j, carry):
        total = kept[far_steps + j]
        for step in range(chips - 1):
            t = step * per_chip + j
            cross_copy(t).wait_recv()
            total = total + cross_in[t].astype(jnp.float32)
        out_ref[pl.ds(pl.multiple_of(j * sub, sub), sub), :] = total
        return carry

    lax.fori_loop(0, per_chip, finish, 0)

    for k in range(chunks):
        near_copy(k).wait_send()
        for step in range(chips):
            own_copy(k, step).wait_send()
        for step in range(chips - 1):
            forward_copy(k, step).wait_send()

    @pl.when(has_onward)
    def _():
        for k in range(chunks):
            far_copy(k).wait_send()

    for t in range(steps):
        half_copy(t).wait_send()
        if t < far_steps:
            cross_copy(t).wait_send()


def on_device(
    n, m,
    images, conv_weight, conv_bias, norm_gain, norm_shift, up_weight, up_bias, down_weight, down_bias,
    layer_scale,
):
    chans, rows, width = images.shape
    pixels = rows * width
    chunks = chans // LANES
    channels, units = up_weight.shape
    chips = n // 2
    sub = LANES
    steps = chips * (chans // sub)
    x = images.reshape(chunks, LANES, rows, width).transpose(0, 2, 3, 1)
    taps = conv_weight.reshape(chunks, LANES, TAPS * TAPS).transpose(0, 2, 1)
    vmem = pl.BlockSpec(memory_space=pltpu.VMEM)
    hbm = pl.BlockSpec(memory_space=pl.ANY)
    bf16, f32 = jnp.bfloat16, jnp.float32
    dma = pltpu.SemaphoreType.DMA
    mixed = pl.pallas_call(
        functools.partial(kernel, n, m),
        out_shape=jax.ShapeDtypeStruct((chans, pixels), f32),
        in_specs=[vmem] * 6 + [hbm] * 2,
        out_specs=vmem,
        scratch_shapes=[
            pltpu.VMEM((channels, units), bf16),
            pltpu.VMEM((channels, units), bf16),
            pltpu.VMEM((chunks, rows, width, LANES), bf16),
            pltpu.VMEM((chunks, HALO, width, LANES), bf16),
            pltpu.VMEM((rows + 2 * HALO, width + 2 * EDGE, LANES), f32),
            pltpu.VMEM((n * chunks, pixels, LANES), bf16),
            pltpu.VMEM((pixels, channels), bf16),
            pltpu.VMEM((pixels, units), bf16),
            pltpu.VMEM((steps, sub, pixels), bf16),
            pltpu.VMEM((steps, sub, pixels), bf16),
            pltpu.VMEM((steps, sub, pixels), f32),
            pltpu.VMEM((steps, sub, pixels), bf16),
            pltpu.VMEM((steps, sub, pixels), bf16),
            dma, dma,
            dma((chunks,)), dma((chunks,)), dma((chunks,)), dma((chunks,)),
            dma((chips * chunks,)), dma((chips * chunks,)), dma((n * chunks,)),
            dma((steps,)), dma((steps,)), dma((steps,)), dma((steps,)),
        ],
        compiler_params=pltpu.CompilerParams(collective_id=0, has_side_effects=True),
    )(
        x, taps, conv_bias.reshape(chunks, 1, LANES), norm_gain.reshape(1, channels),
        norm_shift.reshape(1, channels), up_bias.reshape(1, units), up_weight, down_weight,
    )
    result = images.astype(f32) + (
        layer_scale[:, None] * (mixed + down_bias[:, None])
    ).reshape(chans, rows, width)
    return result.astype(bf16)


def solution(mesh):
    placed = (
        P("pix", "chan", None),
        P("pix", None),
        P("pix"),
        P(),
        P(),
        P(None, "pix"),
        P("pix"),
        P(None, "pix"),
        P("pix"),
        P("pix"),
    )
    return jax.shard_map(
        functools.partial(on_device, mesh.shape["pix"], mesh.shape["chan"]),
        mesh=mesh, in_specs=placed, out_specs=P("pix", "chan", None), check_vma=False,
    )
```

time: 195 us -> 62.6 us (0.32)
  waiting for transfers between devices: 82.9 us -> 0 us
  Pallas kernels: 0 us -> 55.9 us
  other arithmetic: 57.5 us -> 2.49 us
  matrix products: 18.1 us -> 0 us
  between operations: 13.5 us -> 0.05 us
  blocking collectives: 6.55 us -> 0 us
  starting transfers between devices: 5.54 us -> 0 us
  local copies, waits for them, and re-layouts: 8.88 us -> 4 us
    pallas_call x0 -> x1, Pallas kernels: none -> 55.9 us  [on_device(): pl.pallas_call(functools.partial(kernel, n, m), out_shape=jax.ShapeDtypeS...]
    reduce_sum x1 -> x0, other arithmetic: 52.7 us -> none  [on_device(): jnp.sum(values, axis=0)]
    reduce_scatter x1 -> x0, waiting for transfers between devices: 42.7 us -> none  [on_device(): mixed = lax.psum_scatter(terms, 'pix', scatter_dimension=0, tiled=True)]
    all_gather x1 -> x0, waiting for transfers between devices: 24.3 us -> none  [on_device(): gathered = lax.all_gather(normed_local, 'pix', axis=0, tiled=True)]
    dot_general x1 -> x0, matrix products: 18.1 us -> none  [on_device(): terms = jnp.dot(down_weight, hidden, preferred_element_type=jnp.float32)]
    ppermute x2 -> x0, waiting for transfers between devices: 15.8 us -> none  [the longest x1 15.8 us: with_halo(): lax.ppermute(lax.slice_in_dim(block, block.shape[dim] - width, None, axis...]
    psum x1 -> x0, blocking collectives: 6.55 us -> none  [on_device(): lax.psum((jnp.sum(values, axis=0), jnp.sum(values * values, axis=0)), 'pix')]
    ppermute x2 -> x0, starting transfers between devices: 5.31 us -> none  [the longest x1 3.18 us: with_halo(): lax.ppermute(lax.slice_in_dim(block, block.shape[dim] - width, None, axis...]
  transfers between devices with their start and end apart: 4 -> 0, of which waited for: 3 -> 0; matrix products, arithmetic and copies ran while one was open for 3% -> 0% of each run, Pallas kernels for 0% -> 0%
where the time goes in v1:
time: 62.6 us; the launch traced here: 62.4 us
  Pallas kernels  55.9 us (89%)
  local copies, waits for them, and re-layouts  4 us (6%)
  other arithmetic  2.49 us (4%)
    pallas_call x1, Pallas kernels, on_device(): pl.pallas_call(functools.partial(kernel, n, m), out_shape=jax.ShapeDtypeS...  55.9 us
    reshape x1, local copies, waits for them, and re-layouts, on_device(): x = images.reshape(chunks, LANES, rows, width).transpose(0, 2, 3, 1)  2.05 us
    reshape x2, local copies, waits for them, and re-layouts, on_device(): taps = conv_weight.reshape(chunks, LANES, TAPS * TAPS).transpose(0, 2, 1)  1.58 us
    mul x1, other arithmetic, on_device(): layer_scale[:, None] * (mixed + down_bias[:, None])  1.43 us

profile of v1, /device:TPU:3, one launch (start us, length us, event | category | flops | bytes accessed | tf_op | source)
XLA Modules:
  0.0 62.4 jit_solution(14770617062484064948)
XLA Ops:
  0.0 0.9 %reshape.24 = f32[4,128,49]{1,0,2:T(4,128)S(1)} reshape(f32[512,49]{0,1:T(8,128)} %param.11) | data formatting | bytes 200704 | tf_op jit(solution)/shard_map/reshape | solution.py:312
  0.9 0.6 %copy.17 = f32[4,128,49]{1,2,0:T(8,128)} copy(f32[4,128,49]{1,0,2:T(4,128)S(1)} %reshape.24) | data formatting | bytes 200704 | tf_op jit(solution)/shard_map/reshape | solution.py:312
  1.6 2.0 %copy.12 = bf16[4,128,4,128]{1,3,2,0:T(8,128)(2,1)} copy(bf16[4,128,4,128]{3,2,1,0:T(4,128)(2,1)} %bitcast.12) | data formatting | bytes 1048576 | tf_op jit(solution)/shard_map/reshape | solution.py:311
  3.6 0.0 copy-start.1
  3.6 0.0 copy-start.2
  3.6 0.0 copy-start
  3.6 55.9 %shard_map.100 = f32[512,512]{1,0:T(8,128)} custom-call(bf16[4,4,128,128]{3,2,1,0:T(8,128)(2,1)} %bitcast.11, f32[4,49,128]{2,1,0:T(8,128)} %bitcast.13, f32[4,1,128]{2,1,0:T(1,128)} %bitcast.17, f32[1,2048]{1,0:T(1,128)} %bitcast.14, f32[1,2048]{1,0:T(1,128)} %bitcast.15, f32[1,2048]{1,0:T(1,128)} %bitcast.16, bf16[2048,2048]{1,0:T(8,128)(2,1)} %up_hbm.1, ...), custom_call_target="tpu_custom_call" | custom-call | tf_op jit(solution)/shard_map/pallas_call | solution.py:317
  59.5 0.0 copy-done.1
  59.5 0.0 copy-done.2
  59.5 1.4 %add_multiply_fusion = f32[512,512]{1,0:T(8,128)S(1)} fusion(f32[512,512]{1,0:T(8,128)} %shard_map.100, f32[512]{0:T(512)S(1)} %copy-done.1, f32[512]{0:T(512)S(1)} %copy-done.2), kind=kLoop, calls=%fused_computation.1 | loop fusion | flops 524288 | bytes 2101248 | tf_op jit(solution)/shard_map/mul | solution.py:347
  61.0 0.4 reshape.29
  61.3 0.0 copy-done
  61.3 1.1 %add_convert_fusion = bf16[512,4,128]{2,1,0:T(4,128)(2,1)} fusion(f32[512,4,128]{2,1,0:T(4,128)S(1)} %reshape.29, bf16[512,4,128]{2,1,0:T(4,128)(2,1)S(1)} %copy-done), kind=kLoop, calls=%fused_computation | loop fusion | flops 786432 | bytes 2097152 | tf_op jit(solution)/shard_map/convert_element_type | solution.py:349
Async XLA Ops:
  3.6 55.9 %copy-start.1 = (f32[512]{0:T(512)S(1)}, f32[512]{0:T(512)}, u32[]{:S(2)}) copy-start(f32[512]{0:T(512)} %param.18) | copy-start | bytes 6148
  3.6 55.9 %copy-start.2 = (f32[512]{0:T(512)S(1)}, f32[512]{0:T(512)}, u32[]{:S(2)}) copy-start(f32[512]{0:T(512)} %param.19) | copy-start | bytes 6148
  3.6 57.7 %copy-start = (bf16[512,4,128]{2,1,0:T(4,128)(2,1)S(1)}, bf16[512,4,128]{2,1,0:T(4,128)(2,1)}, u32[]{:S(2)}) copy-start(bf16[512,4,128]{2,1,0:T(4,128)(2,1)} %param.10) | copy-start | bytes 1572868

commit v2 on v1

v2 whole, which is shorter than its diff:
```python
import functools

import jax
import jax.numpy as jnp
from jax import lax
from jax.experimental import pallas as pl
from jax.experimental.pallas import tpu as pltpu
from jax.sharding import PartitionSpec as P

MESH = pl.DeviceIdType.MESH
LANES = 128
TAPS = 7
HALO = 3
EDGE = 8
STRIP = 16
PARTS = 2


def kernel(
    n, m, x_ref, weight_ref, cbias_ref, gain_ref, shift_ref, ubias_ref, scale_ref, dbias_ref, up_hbm, down_hbm,
    out_ref,
    up, down, near, far, wide, square, taps, scales, biases, gath, normed, hidden,
    half_out, half_in, kept, cross_out, cross_in,
    up_sem, down_sem, near_send, near_recv, far_send, far_recv,
    gath_send, fwd_send, gath_recv, half_send, half_recv, cross_send, cross_recv,
):
    chunks, rows, width, _ = x_ref.shape
    span = width // PARTS
    pixels = rows * span
    chips = n // 2
    slots = n * chunks
    channels = slots * LANES
    block = channels // n
    sub = half_out.shape[1]
    steps = half_out.shape[0] // PARTS
    per_chip = steps // chips
    far_steps = steps - per_chip
    pix = lax.axis_index("pix")
    chan = lax.axis_index("chan")
    chip, core = pix // 2, pix % 2
    odd = chan % 2
    beside = chan + 1 - 2 * odd
    onward = chan + 2 - 4 * odd
    behind = chan - 2 + 4 * odd
    has_onward = (onward >= 0) & (onward < m)
    has_behind = (behind >= 0) & (behind < m)
    partner = pix + 1 - 2 * core

    def other(step):
        return ((chip + 1 + step) % chips) * 2 + core

    barrier = pltpu.get_barrier_semaphore()

    def greet(to_pix, to_chan):
        pl.semaphore_signal(
            barrier, inc=1, device_id={"pix": to_pix, "chan": to_chan}, device_id_type=MESH
        )

    greet(pix, beside)
    greet(partner, chan)
    for step in range(chips - 1):
        greet(other(step), chan)

    @pl.when(has_onward)
    def _():
        greet(pix, onward)

    @pl.when(has_behind)
    def _():
        greet(pix, behind)

    up_copy = pltpu.make_async_copy(up_hbm, up, up_sem)
    down_copy = pltpu.make_async_copy(down_hbm, down, down_sem)
    pl.semaphore_wait(
        barrier, 1 + chips + has_onward.astype(jnp.int32) + has_behind.astype(jnp.int32)
    )

    def remote(src, dst, send, recv, to_pix, to_chan):
        return pltpu.make_async_remote_copy(
            src_ref=src, dst_ref=dst, send_sem=send, recv_sem=recv,
            device_id={"pix": to_pix, "chan": to_chan}, device_id_type=MESH,
        )

    pieces = [(h, k) for h in range(PARTS) for k in range(chunks)]
    bounds = [0] + [span * (h + 1) + STRIP for h in range(PARTS - 1)] + [width]

    def fresh(h):
        return pl.ds(bounds[h], bounds[h + 1] - bounds[h])

    def near_copy(h, k):
        i = h * chunks + k
        return remote(
            x_ref.at[k, :, fresh(h)], near.at[k, :, fresh(h)], near_send.at[i], near_recv.at[i], pix, beside
        )

    def far_copy(h, k):
        i = h * chunks + k
        return remote(
            near.at[k, pl.ds(1 - odd, HALO), fresh(h)], far.at[k, :, fresh(h)],
            far_send.at[i], far_recv.at[i], pix, onward,
        )

    def own_copy(h, k, step):
        index = h * slots + pix * chunks + k
        to = partner if step == chips - 1 else other(step)
        return remote(
            gath.at[index], gath.at[index], gath_send.at[(step * PARTS + h) * chunks + k],
            gath_recv.at[index], to, chan,
        )

    def arrival(index):
        return remote(gath.at[index], gath.at[index], up_sem, gath_recv.at[index], partner, chan)

    def forward_copy(h, k, step):
        index = h * slots + other(step) * chunks + k
        return remote(
            gath.at[index], gath.at[index], fwd_send.at[(step * PARTS + h) * chunks + k],
            gath_recv.at[index], partner, chan,
        )

    for h, k in pieces:
        near_copy(h, k).start()
    up_copy.start()
    down_copy.start()

    wide[...] = jnp.zeros_like(wide)

    @pl.when(jnp.logical_not(has_behind))
    def _():
        far[...] = jnp.zeros_like(far)

    square[...] = jnp.zeros_like(square)
    for k in range(chunks):
        square[:, : TAPS * TAPS] = weight_ref[k * LANES : (k + 1) * LANES, :]
        taps[k] = square[...].T
    for j in range(per_chip):
        lanes = slice(j * sub, (j + 1) * sub)
        scales[j] = jnp.broadcast_to(scale_ref[:, lanes], (sub, sub)).T
        biases[j] = jnp.broadcast_to(dbias_ref[:, lanes], (sub, sub)).T

    def pass_on(h, k):
        near_copy(h, k).wait_recv()

        @pl.when(has_onward)
        def _():
            far_copy(h, k).start()

    def filter_piece(h, k):
        @pl.when(has_behind)
        def _():
            far_copy(h, k).wait_recv()

        low = max(span * h - STRIP, 0)
        high = bounds[h + 1]
        inner = slice(EDGE + low, EDGE + high)
        some = slice(low, high)
        wide[HALO : HALO + rows, inner, :] = x_ref[k, :, some].astype(jnp.float32)
        wide[pl.ds((HALO + rows) * (1 - odd), HALO), inner, :] = near[
            k, pl.ds(odd * (rows - HALO), HALO), some
        ].astype(jnp.float32)
        wide[pl.ds((HALO + rows) * odd, HALO), inner, :] = far[k, :, some].astype(jnp.float32)
        bias = cbias_ref[k]
        own = h * slots + pix * chunks + k

        def strip(s, carry):
            place = pl.multiple_of(s * STRIP, STRIP)
            sums = [jnp.zeros((STRIP, LANES), jnp.float32) for _ in range(rows)]
            for b in range(TAPS):
                for i in range(rows + TAPS - 1):
                    piece = wide[i, pl.ds(place + (span * h + EDGE - HALO + b), STRIP), :]
                    for o in range(rows):
                        a = i - o
                        if 0 <= a < TAPS:
                            tap = a * TAPS + b
                            sums[o] = sums[o] + taps[k, tap : tap + 1, :] * piece
            for o in range(rows):
                gath[own, pl.ds(pl.multiple_of(o * span + place, STRIP), STRIP), :] = (
                    sums[o] + bias
                ).astype(jnp.bfloat16)
            return carry

        lax.fori_loop(0, span // STRIP, strip, 0)
        for step in range(chips):
            own_copy(h, k, step).start()

    def relay(h, k):
        for step in range(chips - 1):
            arrival(h * slots + other(step) * chunks + k).wait_recv()
            forward_copy(h, k, step).start()

    def settle(h):
        def one(k, carry):
            arrival(h * slots + partner * chunks + k).wait_recv()
            for step in range(chips - 1):
                mate = other(step) + 1 - 2 * core
                arrival(h * slots + mate * chunks + k).wait_recv()
            return carry

        lax.fori_loop(0, chunks, one, 0)

    count = len(pieces)
    early = chunks
    lag = 3
    for i in range(count + 1):
        if i < count:
            pass_on(*pieces[i])
        if i >= 1:
            filter_piece(*pieces[i - 1])
        if i >= lag and i - lag < early:
            relay(*pieces[i - lag])
    for i in range(max(count + 1 - lag, 0), early):
        relay(*pieces[i])

    band = 64

    def normalise(h):
        def one(s, carry):
            here = pl.ds(pl.multiple_of(s * band, band), band)
            first = jnp.zeros((band, LANES), jnp.float32)
            second = jnp.zeros((band, LANES), jnp.float32)
            for q in range(slots):
                v = gath[h * slots + q, here, :].astype(jnp.float32)
                first = first + v
                second = second + v * v
            mean = jnp.sum(first, axis=1, keepdims=True) / channels
            var = jnp.sum(second, axis=1, keepdims=True) / channels - mean * mean
            scale = lax.rsqrt(var + 1e-06)
            for q in range(slots):
                lanes = slice(q * LANES, (q + 1) * LANES)
                v = gath[h * slots + q, here, :].astype(jnp.float32)
                normed[here, lanes] = (
                    (v - mean) * scale * gain_ref[:, lanes] + shift_ref[:, lanes]
                ).astype(jnp.bfloat16)
            return carry

        lax.fori_loop(0, pixels // band, one, 0)

    units = up.shape[1]
    tile = 256
    pair = 2

    def gelu(v):
        return 0.5 * v * (1.0 + jnp.tanh(0.7978845608 * (v + 0.044715 * (v * v * v))))

    def expand(h):
        def one(s, carry):
            if h + 1 < PARTS:
                @pl.when(s < chunks)
                def _():
                    relay(h + 1, s)

            cols = [
                pl.ds(pl.multiple_of(s * (pair * tile), pair * tile) + u * tile, tile) for u in range(pair)
            ]
            sums = [
                jnp.dot(normed[...], up[:, c], preferred_element_type=jnp.float32) + ubias_ref[:, c]
                for c in cols
            ]
            for c, v in zip(cols, sums):
                hidden[:, c] = gelu(v).astype(jnp.bfloat16)
            return carry

        rounds = units // (pair * tile)
        lax.fori_loop(0, rounds, one, 0)
        if h + 1 < PARTS:
            for k in range(rounds, chunks):
                relay(h + 1, k)

    def half_copy(h, t):
        i = h * steps + t
        return remote(half_out.at[i], half_in.at[i], half_send.at[i], half_recv.at[i], partner, chan)

    def cross_copy(h, t):
        i = h * steps + t
        return remote(
            cross_out.at[i], cross_in.at[i], cross_send.at[i], cross_recv.at[i],
            other(t // per_chip), chan,
        )

    def contract(start):
        part = down[pl.ds(pl.multiple_of(start, sub), sub), :]
        return lax.dot_general(
            part, hidden[...], (((1,), (1,)), ((), ())), preferred_element_type=jnp.float32
        )

    def combine(h, t):
        half_copy(h, t).wait_recv()
        i = h * steps + t

        @pl.when(t < far_steps)
        def _():
            cross_out[i] = (kept[i] + half_in[i].astype(jnp.float32)).astype(jnp.bfloat16)
            cross_copy(h, t).start()

        @pl.when(t >= far_steps)
        def _():
            kept[i] = kept[i] + half_in[i].astype(jnp.float32)

    def reduce(h):
        def one(t, carry):
            @pl.when(t < steps)
            def _():
                owner = other(t // per_chip)
                away = owner + 1 - 2 * core
                row = (t % per_chip) * sub
                half_out[h * steps + t] = contract(away * block + row).astype(jnp.bfloat16)
                half_copy(h, t).start()
                kept[h * steps + t] = contract(owner * block + row)

            @pl.when(t >= 1)
            def _():
                combine(h, t - 1)

            return carry

        lax.fori_loop(0, steps + 1, one, 0)

    for h in range(PARTS):
        settle(h)
        normalise(h)
        if h == 0:
            up_copy.wait()
        expand(h)
        if h == 0:
            down_copy.wait()
        reduce(h)

    def finish(j, carry):
        totals = []
        for h in range(PARTS):
            total = kept[h * steps + far_steps + j]
            for step in range(chips - 1):
                t = step * per_chip + j
                cross_copy(h, t).wait_recv()
                total = total + cross_in[h * steps + t].astype(jnp.float32)
            totals.append(total)
        here = pl.ds(pl.multiple_of(j * sub, sub), sub)
        for r in range(rows):
            line = jnp.concatenate([total[:, r * span : (r + 1) * span] for total in totals], axis=1)
            out_ref[here, r * width : (r + 1) * width] = scales[j] * (line + biases[j])
        return carry

    lax.fori_loop(0, per_chip, finish, 0)

    for h, k in pieces:
        near_copy(h, k).wait_send()
        for step in range(chips):
            own_copy(h, k, step).wait_send()
        for step in range(chips - 1):
            forward_copy(h, k, step).wait_send()

    @pl.when(has_onward)
    def _():
        for h, k in pieces:
            far_copy(h, k).wait_send()

    for h in range(PARTS):
        def sent(t, carry):
            half_copy(h, t).wait_send()

            @pl.when(t < far_steps)
            def _():
                cross_copy(h, t).wait_send()

            return carry

        lax.fori_loop(0, steps, sent, 0)


def on_device(
    n, m,
    images, conv_weight, conv_bias, norm_gain, norm_shift, up_weight, up_bias, down_weight, down_bias,
    layer_scale,
):
    chans, rows, width = images.shape
    pixels = rows * width
    chunks = chans // LANES
    channels, units = up_weight.shape
    chips = n // 2
    sub = LANES
    steps = chips * (chans // sub)
    x = images.reshape(chunks, LANES, rows, width).transpose(0, 2, 3, 1)
    span = width // PARTS
    part = rows * span
    vmem = pl.BlockSpec(memory_space=pltpu.VMEM)
    hbm = pl.BlockSpec(memory_space=pl.ANY)
    bf16, f32 = jnp.bfloat16, jnp.float32
    dma = pltpu.SemaphoreType.DMA
    mixed = pl.pallas_call(
        functools.partial(kernel, n, m),
        out_shape=jax.ShapeDtypeStruct((chans, pixels), f32),
        in_specs=[vmem] * 8 + [hbm] * 2,
        out_specs=vmem,
        scratch_shapes=[
            pltpu.VMEM((channels, units), bf16),
            pltpu.VMEM((channels, units), bf16),
            pltpu.VMEM((chunks, rows, width, LANES), bf16),
            pltpu.VMEM((chunks, HALO, width, LANES), bf16),
            pltpu.VMEM((rows + 2 * HALO, width + 2 * EDGE, LANES), f32),
            pltpu.VMEM((LANES, LANES), f32),
            pltpu.VMEM((chunks, LANES, LANES), f32),
            pltpu.VMEM((chans // sub, sub, sub), f32),
            pltpu.VMEM((chans // sub, sub, sub), f32),
            pltpu.VMEM((PARTS * n * chunks, part, LANES), bf16),
            pltpu.VMEM((part, channels), bf16),
            pltpu.VMEM((part, units), bf16),
            pltpu.VMEM((PARTS * steps, sub, part), bf16),
            pltpu.VMEM((PARTS * steps, sub, part), bf16),
            pltpu.VMEM((PARTS * steps, sub, part), f32),
            pltpu.VMEM((PARTS * steps, sub, part), bf16),
            pltpu.VMEM((PARTS * steps, sub, part), bf16),
            dma, dma,
            dma((PARTS * chunks,)), dma((PARTS * chunks,)), dma((PARTS * chunks,)), dma((PARTS * chunks,)),
            dma((PARTS * chips * chunks,)), dma((PARTS * chips * chunks,)), dma((PARTS * n * chunks,)),
            dma((PARTS * steps,)), dma((PARTS * steps,)), dma((PARTS * steps,)), dma((PARTS * steps,)),
        ],
        compiler_params=pltpu.CompilerParams(collective_id=0, has_side_effects=True),
    )(
        x, conv_weight, conv_bias.reshape(chunks, 1, LANES), norm_gain.reshape(1, channels),
        norm_shift.reshape(1, channels), up_bias.reshape(1, units), layer_scale.reshape(1, chans),
        down_bias.reshape(1, chans), up_weight, down_weight,
    )
    return (images.astype(f32) + mixed.reshape(chans, rows, width)).astype(bf16)


def solution(mesh):
    placed = (
        P("pix", "chan", None),
        P("pix", None),
        P("pix"),
        P(),
        P(),
        P(None, "pix"),
        P("pix"),
        P(None, "pix"),
        P("pix"),
        P("pix"),
    )
    return jax.shard_map(
        functools.partial(on_device, mesh.shape["pix"], mesh.shape["chan"]),
        mesh=mesh, in_specs=placed, out_specs=P("pix", "chan", None), check_vma=False,
    )
```

time: 62.6 us -> 68.7 us (1.097)
  Pallas kernels: 55.9 us -> 62 us
  other arithmetic: 2.49 us -> 1.06 us
  local copies, waits for them, and re-layouts: 4 us -> 5.35 us
    pallas_call x1, Pallas kernels: 55.9 us -> 62 us  [on_device(): pl.pallas_call(functools.partial(kernel, n, m), out_shape=jax.ShapeDtypeS...]
    unnamed x6 -> x3, local copies, waits for them, and re-layouts: 0.01 us -> 1.74 us
    mul x1 -> x0, other arithmetic: 1.43 us -> none  [on_device(): layer_scale[:, None] * (mixed + down_bias[:, None])]
    reshape x3 -> x1, local copies, waits for them, and re-layouts: 1.94 us -> 1.56 us  [on_device(): return (images.astype(f32) + mixed.reshape(chans, rows, width)).astype(bf16)]
where the time goes in v2:
time: 68.7 us; the launch traced here: 68.4 us
  Pallas kernels  62 us (90%)
  local copies, waits for them, and re-layouts  5.35 us (8%)
  other arithmetic  1.06 us (2%)
    pallas_call x1, Pallas kernels, on_device(): pl.pallas_call(functools.partial(kernel, n, m), out_shape=jax.ShapeDtypeS...  62 us
    reshape x1, local copies, waits for them, and re-layouts, on_device(): x = images.reshape(chunks, LANES, rows, width).transpose(0, 2, 3, 1)  2.05 us
    unnamed x3, local copies, waits for them, and re-layouts  1.74 us
    reshape x1, local copies, waits for them, and re-layouts, on_device(): return (images.astype(f32) + mixed.reshape(chans, rows, width)).astype(bf16)  1.56 us

profile of v2, /device:TPU:3, one launch (start us, length us, event | category | flops | bytes accessed | tf_op | source)
XLA Modules:
  0.0 68.4 jit_solution(12838447713571565070)
XLA Ops:
  0.0 1.7 %copy.14.weight_ref = f32[512,49]{1,0:T(8,128)} copy(f32[512,49]{0,1:T(8,128)} %param.11) | data formatting | bytes 200704 | tf_op args[1]
  1.7 2.0 %copy.13 = bf16[4,128,4,128]{1,3,2,0:T(8,128)(2,1)} copy(bf16[4,128,4,128]{3,2,1,0:T(4,128)(2,1)} %bitcast.9) | data formatting | bytes 1048576 | tf_op jit(solution)/shard_map/reshape | solution.py:382
  3.8 0.0 copy-start
  3.8 62.0 %shard_map.100 = f32[512,512]{1,0:T(8,128)} custom-call(bf16[4,4,128,128]{3,2,1,0:T(8,128)(2,1)} %bitcast.8, f32[512,49]{1,0:T(8,128)} %copy.14.weight_ref, f32[4,1,128]{2,1,0:T(1,128)} %bitcast.13, f32[1,2048]{1,0:T(1,128)} %bitcast.10, f32[1,2048]{1,0:T(1,128)} %bitcast.11, f32[1,2048]{1,0:T(1,128)} %bitcast.12, f32[1,512]{1,0:T(1,128)} %bitcast.14, ...), custom_call_target="tpu_custom_call" | custom-call | tf_op jit(solution)/shard_map/pallas_call | solution.py:389
  65.8 1.6 %reshape.31 = f32[512,4,128]{2,1,0:T(4,128)S(1)} reshape(f32[512,512]{1,0:T(8,128)} %shard_map.100) | data formatting | bytes 2097152 | tf_op jit(solution)/shard_map/reshape | solution.py:423
  67.4 0.0 copy-done
  67.4 1.1 %add_convert_fusion = bf16[512,4,128]{2,1,0:T(4,128)(2,1)} fusion(f32[512,4,128]{2,1,0:T(4,128)S(1)} %reshape.31, bf16[512,4,128]{2,1,0:T(4,128)(2,1)S(1)} %copy-done), kind=kLoop, calls=%fused_computation | loop fusion | flops 786432 | bytes 2097152 | tf_op jit(solution)/shard_map/convert_element_type | solution.py:423
Async XLA Ops:
  3.8 63.6 %copy-start = (bf16[512,4,128]{2,1,0:T(4,128)(2,1)S(1)}, bf16[512,4,128]{2,1,0:T(4,128)(2,1)}, u32[]{:S(2)}) copy-start(bf16[512,4,128]{2,1,0:T(4,128)(2,1)} %param.10) | copy-start | bytes 1572868

commit v3 on v2

--- a/solution.py
+++ b/solution.py
@@ -13,13 +13,14 @@
 HALO = 3
 EDGE = 8
 STRIP = 16
-PARTS = 2
+PARTS = 1
+GROUP = 2
 
 
 def kernel(
     n, m, x_ref, weight_ref, cbias_ref, gain_ref, shift_ref, ubias_ref, scale_ref, dbias_ref, up_hbm, down_hbm,
     out_ref,
-    up, down, near, far, wide, square, taps, scales, biases, gath, normed, hidden,
+    up, down, near, far, wide, residual, scales, biases, gath, normed, hidden,
     half_out, half_in, kept, cross_out, cross_in,
     up_sem, down_sem, near_send, near_recv, far_send, far_recv,
     gath_send, fwd_send, gath_recv, half_send, half_recv, cross_send, cross_recv,
@@ -129,14 +130,15 @@
     def _():
         far[...] = jnp.zeros_like(far)
 
-    square[...] = jnp.zeros_like(square)
     for k in range(chunks):
-        square[:, : TAPS * TAPS] = weight_ref[k * LANES : (k + 1) * LANES, :]
-        taps[k] = square[...].T
+        for row in range(rows):
+            residual[k * LANES : (k + 1) * LANES, row * width : (row + 1) * width] = (
+                x_ref[k, row].astype(jnp.float32).T
+            )
     for j in range(per_chip):
         lanes = slice(j * sub, (j + 1) * sub)
-        scales[j] = jnp.broadcast_to(scale_ref[:, lanes], (sub, sub)).T
-        biases[j] = jnp.broadcast_to(dbias_ref[:, lanes], (sub, sub)).T
+        scales[j] = jnp.broadcast_to(scale_ref[:, lanes], (width, sub)).T
+        biases[j] = jnp.broadcast_to(dbias_ref[:, lanes], (width, sub)).T
 
     def pass_on(h, k):
         near_copy(h, k).wait_recv()
@@ -172,7 +174,7 @@
                         a = i - o
                         if 0 <= a < TAPS:
                             tap = a * TAPS + b
-                            sums[o] = sums[o] + taps[k, tap : tap + 1, :] * piece
+                            sums[o] = sums[o] + weight_ref[tap : tap + 1, k * LANES : (k + 1) * LANES] * piece
             for o in range(rows):
                 gath[own, pl.ds(pl.multiple_of(o * span + place, STRIP), STRIP), :] = (
                     sums[o] + bias
@@ -337,7 +339,10 @@
         here = pl.ds(pl.multiple_of(j * sub, sub), sub)
         for r in range(rows):
             line = jnp.concatenate([total[:, r * span : (r + 1) * span] for total in totals], axis=1)
-            out_ref[here, r * width : (r + 1) * width] = scales[j] * (line + biases[j])
+            columns = slice(r * width, (r + 1) * width)
+            out_ref[here, columns] = (
+                residual[here, columns] + scales[j] * (line + biases[j])
+            ).astype(out_ref.dtype)
         return carry
 
     lax.fori_loop(0, per_chip, finish, 0)
@@ -377,7 +382,7 @@
     chunks = chans // LANES
     channels, units = up_weight.shape
     chips = n // 2
-    sub = LANES
+    sub = min(GROUP * LANES, chans)
     steps = chips * (chans // sub)
     x = images.reshape(chunks, LANES, rows, width).transpose(0, 2, 3, 1)
     span = width // PARTS
@@ -386,9 +391,9 @@
     hbm = pl.BlockSpec(memory_space=pl.ANY)
     bf16, f32 = jnp.bfloat16, jnp.float32
     dma = pltpu.SemaphoreType.DMA
-    mixed = pl.pallas_call(
+    result = pl.pallas_call(
         functools.partial(kernel, n, m),
-        out_shape=jax.ShapeDtypeStruct((chans, pixels), f32),
+        out_shape=jax.ShapeDtypeStruct((chans, pixels), bf16),
         in_specs=[vmem] * 8 + [hbm] * 2,
         out_specs=vmem,
         scratch_shapes=[
@@ -397,10 +402,9 @@
             pltpu.VMEM((chunks, rows, width, LANES), bf16),
             pltpu.VMEM((chunks, HALO, width, LANES), bf16),
             pltpu.VMEM((rows + 2 * HALO, width + 2 * EDGE, LANES), f32),
-            pltpu.VMEM((LANES, LANES), f32),
-            pltpu.VMEM((chunks, LANES, LANES), f32),
-            pltpu.VMEM((chans // sub, sub, sub), f32),
-            pltpu.VMEM((chans // sub, sub, sub), f32),
+            pltpu.VMEM((chans, pixels), f32),
+            pltpu.VMEM((chans // sub, sub, width), f32),
+            pltpu.VMEM((chans // sub, sub, width), f32),
             pltpu.VMEM((PARTS * n * chunks, part, LANES), bf16),
             pltpu.VMEM((part, channels), bf16),
             pltpu.VMEM((part, units), bf16),
@@ -416,11 +420,11 @@
         ],
         compiler_params=pltpu.CompilerParams(collective_id=0, has_side_effects=True),
     )(
-        x, conv_weight, conv_bias.reshape(chunks, 1, LANES), norm_gain.reshape(1, channels),
+        x, conv_weight.T, conv_bias.reshape(chunks, 1, LANES), norm_gain.reshape(1, channels),
         norm_shift.reshape(1, channels), up_bias.reshape(1, units), layer_scale.reshape(1, chans),
         down_bias.reshape(1, chans), up_weight, down_weight,
     )
-    return (images.astype(f32) + mixed.reshape(chans, rows, width)).astype(bf16)
+    return result.reshape(chans, rows, width)
 
 
 def solution(mesh):

time: 68.7 us -> 56.8 us (0.83)
  Pallas kernels: 62 us -> 52.5 us
  local copies, waits for them, and re-layouts: 5.35 us -> 4.01 us
  other arithmetic: 1.06 us -> 0 us
    pallas_call x1, Pallas kernels: 62 us -> 52.5 us  [on_device(): pl.pallas_call(functools.partial(kernel, n, m), out_shape=jax.ShapeDtypeS...]
    unnamed x3 -> x0, local copies, waits for them, and re-layouts: 1.74 us -> none
    convert_element_type x1 -> x0, other arithmetic: 1.06 us -> none  [on_device(): return (images.astype(f32) + mixed.reshape(chans, rows, width)).astype(bf16)]
where the time goes in v3:
time: 56.8 us; the launch traced here: 56.5 us
  Pallas kernels  52.5 us (92%)
  local copies, waits for them, and re-layouts  4.01 us (7%)
    pallas_call x1, Pallas kernels, on_device(): pl.pallas_call(functools.partial(kernel, n, m), out_shape=jax.ShapeDtypeS...  52.5 us
    reshape x1, local copies, waits for them, and re-layouts, on_device(): x = images.reshape(chunks, LANES, rows, width).transpose(0, 2, 3, 1)  2.05 us
    reshape x1, local copies, waits for them, and re-layouts, on_device(): return result.reshape(chans, rows, width)  1.96 us

profile of v3, /device:TPU:3, one launch (start us, length us, event | category | flops | bytes accessed | tf_op | source)
XLA Modules:
  0.0 56.5 jit_solution(18408501630912565412)
XLA Ops:
  0.0 2.0 %copy.12 = bf16[4,128,4,128]{1,3,2,0:T(8,128)(2,1)} copy(bf16[4,128,4,128]{3,2,1,0:T(4,128)(2,1)} %bitcast.10) | data formatting | bytes 1048576 | tf_op jit(solution)/shard_map/reshape | solution.py:387
  2.0 52.5 %shard_map.100 = bf16[512,512]{1,0:T(8,128)(2,1)} custom-call(bf16[4,4,128,128]{3,2,1,0:T(8,128)(2,1)} %bitcast.9, f32[49,512]{1,0:T(8,128)} %bitcast.11, f32[4,1,128]{2,1,0:T(1,128)} %bitcast.15, f32[1,2048]{1,0:T(1,128)} %bitcast.12, f32[1,2048]{1,0:T(1,128)} %bitcast.13, f32[1,2048]{1,0:T(1,128)} %bitcast.14, f32[1,512]{1,0:T(1,128)} %bitcast.16, ...), custom_call_target="tpu_custom_call" | custom-call | tf_op jit(solution)/shard_map/pallas_call | solution.py:394
  54.6 2.0 %reshape.31 = bf16[512,4,128]{2,1,0:T(4,128)(2,1)} reshape(bf16[512,512]{1,0:T(8,128)(2,1)} %shard_map.100) | data formatting | bytes 1048576 | tf_op jit(solution)/shard_map/reshape | solution.py:427

commit v4 on v3

--- a/solution.py
+++ b/solution.py
@@ -239,7 +239,7 @@
 
     units = up.shape[1]
     tile = 256
-    pair = 2
+    pair = max(min(4, units // tile), 1)
 
     def gelu(v):
         return 0.5 * v * (1.0 + jnp.tanh(0.7978845608 * (v + 0.044715 * (v * v * v))))
@@ -307,11 +307,15 @@
                 row = (t % per_chip) * sub
                 half_out[h * steps + t] = contract(away * block + row).astype(jnp.bfloat16)
                 half_copy(h, t).start()
-                kept[h * steps + t] = contract(owner * block + row)
 
             @pl.when(t >= 1)
             def _():
                 combine(h, t - 1)
+
+            @pl.when(t < steps)
+            def _():
+                owner = other(t // per_chip)
+                kept[h * steps + t] = contract(owner * block + (t % per_chip) * sub)
 
             return carry
 

time: 56.8 us -> 56.5 us (level)
  no operation moved by 1% of the time
where the time goes in v4:
time: 56.5 us; the launch traced here: 56 us
  Pallas kernels  52 us (92%)
  local copies, waits for them, and re-layouts  4.01 us (7%)
    pallas_call x1, Pallas kernels, on_device(): pl.pallas_call(functools.partial(kernel, n, m), out_shape=jax.ShapeDtypeS...  52 us
    reshape x1, local copies, waits for them, and re-layouts, on_device(): x = images.reshape(chunks, LANES, rows, width).transpose(0, 2, 3, 1)  2.05 us
    reshape x1, local copies, waits for them, and re-layouts, on_device(): return result.reshape(chans, rows, width)  1.96 us

profile of v4, /device:TPU:3, one launch (start us, length us, event | category | flops | bytes accessed | tf_op | source)
XLA Modules:
  0.0 56.0 jit_solution(2740912873709021642)
XLA Ops:
  0.0 2.0 %copy.12 = bf16[4,128,4,128]{1,3,2,0:T(8,128)(2,1)} copy(bf16[4,128,4,128]{3,2,1,0:T(4,128)(2,1)} %bitcast.10) | data formatting | bytes 1048576 | tf_op jit(solution)/shard_map/reshape | solution.py:391
  2.0 52.0 %shard_map.100 = bf16[512,512]{1,0:T(8,128)(2,1)} custom-call(bf16[4,4,128,128]{3,2,1,0:T(8,128)(2,1)} %bitcast.9, f32[49,512]{1,0:T(8,128)} %bitcast.11, f32[4,1,128]{2,1,0:T(1,128)} %bitcast.15, f32[1,2048]{1,0:T(1,128)} %bitcast.12, f32[1,2048]{1,0:T(1,128)} %bitcast.13, f32[1,2048]{1,0:T(1,128)} %bitcast.14, f32[1,512]{1,0:T(1,128)} %bitcast.16, ...), custom_call_target="tpu_custom_call" | custom-call | tf_op jit(solution)/shard_map/pallas_call | solution.py:398
  54.1 2.0 %reshape.31 = bf16[512,4,128]{2,1,0:T(4,128)(2,1)} reshape(bf16[512,512]{1,0:T(8,128)(2,1)} %shard_map.100) | data formatting | bytes 1048576 | tf_op jit(solution)/shard_map/reshape | solution.py:431
